TPU v7x, 32 devices: a whole 2x2x4 slice. The times are simulated.
32 devices in a mesh: tm: 8 (over y, x, core), space: 4 (over z).
Axes of the slice: x: 2, y: 2, z: 4, core: 2. Of those that a mesh axis runs over, the one named last changes fastest.
Arguments:
- frames: bfloat16 [128, 256, 768], P('tm', 'space'), may hold values from -6 to 6
- gain_time: float32 [768], replicated, may hold values from 0.25 to 1.75
- wq_time: bfloat16 [768, 768], replicated, may hold values from -6 to 6
- wkv_time: bfloat16 [768, 512], replicated, may hold values from -6 to 6
- wo_time: bfloat16 [768, 768], replicated, may hold values from -0.21875 to 0.21875
- gain_space: float32 [768], replicated, may hold values from 0.25 to 1.75
- wq_space: bfloat16 [768, 768], replicated, may hold values from -6 to 6
- wkv_space: bfloat16 [768, 512], replicated, may hold values from -6 to 6
- wo_space: bfloat16 [768, 768], replicated, may hold values from -0.21875 to 0.21875
- gain_mlp: float32 [768], replicated, may hold values from 0.25 to 1.75
- w_in: bfloat16 [768, 3072], replicated, may hold values from -0.21875 to 0.21875
- w_out: bfloat16 [3072, 768], replicated, may hold values from -0.109375 to 0.109375
Outputs:
- encoded: bfloat16 [128, 256, 768], P('tm', 'space')
All inputs are finite; a program needn't handle non-finite values.
Results may differ from a plain program's by a relative error of at most 0.025.
The roundings to bfloat16 on the way count: a program that leaves them out, or rounds other values in their place, can miss the bound.
Values may be sent and summed in bfloat16 or wider, within the bound.
A program may use at most 192 MiB of HBM per device.

v0:
```python
import jax
import jax.numpy as jnp
from jax import lax
from jax.sharding import PartitionSpec as P

HEADS = 12
KV_HEADS = 4
HEAD = 64
WINDOW = 8


def extended(x, sides, width):
    for axis, dim in sides:
        size, length = (lax.axis_size(axis), x.shape[dim])
        up = [(i, (i + 1) % size) for i in range(size - 1)]
        down = [(j, i) for i, j in up]
        last = lax.slice_in_dim(x, length - width, length, axis=dim)
        leading = lax.slice_in_dim(x, 0, width, axis=dim)
        before = lax.ppermute(last, axis, up)
        after = lax.ppermute(leading, axis, down)
        x = jnp.concatenate([before, x, after], axis=dim)
    return x


def layer_norm(x, gain):
    xf = x.astype(jnp.float32)
    mean = jnp.mean(xf, axis=-1, keepdims=True)
    var = jnp.mean((xf - mean) * (xf - mean), axis=-1, keepdims=True)
    return ((xf - mean) * lax.rsqrt(var + 1e-06) * gain).astype(jnp.bfloat16)


def project(a, w):
    flat = a.reshape(-1, a.shape[-1])
    return jnp.dot(flat, w, preferred_element_type=jnp.float32).reshape(
        a.shape[:-1] + (w.shape[1],)
    )


def banded_time(queries, padded, valid):
    group = HEADS // KV_HEADS
    count = queries.shape[0]
    patches = queries.shape[1]
    extent = padded.shape[0]
    q_heads = queries.reshape(count, patches, KV_HEADS, group, HEAD)
    k_heads = padded[..., : KV_HEADS * HEAD].reshape(extent, patches, KV_HEADS, HEAD)
    v_heads = padded[..., KV_HEADS * HEAD :].reshape(extent, patches, KV_HEADS, HEAD)
    scores = jnp.einsum(
        "tpgrd,spgd->pgtrs", q_heads, k_heads, preferred_element_type=jnp.float32
    ) / jnp.sqrt(jnp.float32(HEAD))
    scores = jnp.where(valid[:, None, :], scores, jnp.float32(-1e30))
    top = jnp.max(scores, axis=-1, keepdims=True)
    expo = jnp.exp(scores - top)
    weights = (expo / jnp.sum(expo, axis=-1, keepdims=True)).astype(jnp.bfloat16)
    out = jnp.einsum("pgtrs,spgd->tpgrd", weights, v_heads, preferred_element_type=jnp.float32)
    return out.reshape(count, patches, HEADS * HEAD).astype(jnp.bfloat16)


def attend_space(query, keyvals):
    group = HEADS // KV_HEADS
    patches = query.shape[0]
    count = keyvals.shape[0]
    q_heads = query.reshape(patches, KV_HEADS, group, HEAD)
    k_heads = keyvals[:, : KV_HEADS * HEAD].reshape(count, KV_HEADS, HEAD)
    v_heads = keyvals[:, KV_HEADS * HEAD :].reshape(count, KV_HEADS, HEAD)
    scores = jnp.einsum(
        "pgrd,kgd->grpk", q_heads, k_heads, preferred_element_type=jnp.float32
    ) / jnp.sqrt(jnp.float32(HEAD))
    top = jnp.max(scores, axis=-1, keepdims=True)
    expo = jnp.exp(scores - top)
    weights = (expo / jnp.sum(expo, axis=-1, keepdims=True)).astype(jnp.bfloat16)
    out = jnp.einsum("grpk,kgd->pgrd", weights, v_heads, preferred_element_type=jnp.float32)
    return out.reshape(patches, HEADS * HEAD).astype(jnp.bfloat16)


def body(
    frames,
    gain_time,
    wq_time,
    wkv_time,
    wo_time,
    gain_space,
    wq_space,
    wkv_space,
    wo_space,
    gain_mlp,
    w_in,
    w_out,
):
    count = frames.shape[0]
    normed = layer_norm(frames, gain_time)
    queries = project(normed, wq_time).astype(jnp.bfloat16)
    keyvals = project(normed, wkv_time).astype(jnp.bfloat16)
    padded = extended(keyvals, (("tm", 0),), WINDOW)
    extent = padded.shape[0]
    first = lax.axis_index("tm") * count
    total = count * lax.axis_size("tm")
    query_pos = jnp.arange(count, dtype=jnp.int32)[:, None]
    key_pos = jnp.arange(extent, dtype=jnp.int32)[None, :] - WINDOW
    global_key = first + key_pos
    valid = (jnp.abs(key_pos - query_pos) <= WINDOW) & (global_key >= 0) & (global_key < total)
    attended = banded_time(queries, padded, valid)
    after_time = (frames.astype(jnp.float32) + project(attended, wo_time)).astype(jnp.bfloat16)
    normed = layer_norm(after_time, gain_space)
    queries = project(normed, wq_space).astype(jnp.bfloat16)
    keyvals = project(normed, wkv_space).astype(jnp.bfloat16)
    gathered = lax.all_gather(keyvals, "space", axis=1, tiled=True)
    attended = jax.vmap(attend_space)(queries, gathered)
    after_space = (after_time.astype(jnp.float32) + project(attended, wo_space)).astype(
        jnp.bfloat16
    )
    normed = layer_norm(after_space, gain_mlp)
    hidden = jax.nn.gelu(project(normed, w_in), approximate=True).astype(jnp.bfloat16)
    return (after_space.astype(jnp.float32) + project(hidden, w_out)).astype(jnp.bfloat16)


def solution(mesh):
    in_specs = (P("tm", "space", None), P(), P(), P(), P(), P(), P(), P(), P(), P(), P(), P())
    out_specs = P("tm", "space", None)
    return jax.shard_map(body, mesh=mesh, in_specs=in_specs, out_specs=out_specs, check_vma=False)
```

profile of v0, /device:TPU:0, one launch (start us, length us, event | category | flops | bytes accessed | tf_op | source)
XLA Modules:
  0.0 242.6 jit_solution(12706470925719395757)
XLA Ops:
  8.4 2.0 fusion.35
  13.4 3.2 %collective-permute-start = (bf16[8,64,512]{2,1,0:T(8,128)(2,1)}, bf16[8,64,512]{2,1,0:T(8,128)(2,1)}, u32[]{:S(2)}, u32[]{:S(2)}) collective-permute-start(bf16[8,64,512]{2,1,0:T(8,128)(2,1)} %get-tuple-element.9), channel_id=1, source_target_pairs={{0,4},{4,8},{8,12},{12,16},{16,20},{20,24},{24,28},{1,5},{5,9},{9,... | collective-permute-start | bytes 1572872 | tf_op jit(solution)/shard_map/ppermute | solution.py:19
  17.8 2.7 %convolution_convert_fusion.1 = bf16[16,64,768]{2,1,0:T(8,128)(2,1)} fusion(bf16[768,768]{1,0:T(8,128)(2,1)S(1)} %copy-done.11, bf16[16,64,768]{2,1,0:T(8,128)(2,1)S(1)} %copy-done.2, f32[768]{0:T(1024)S(1)} %copy-done.14, f32[16,64]{1,0:T(8,128)S(1)} %add_rsqrt_fusion.2, f32[16,64]{1,0:T(8,128)S(1)} %broadcast_multiply_fusion.2), kind=kOutput, calls=%fused_computation.69 | convolution fusion | flops 1212678144 | bytes 4336640 | tf_op jit(solution)/shard_map/dot_general | solution.py:34
  20.5 9.1 %reshape.113 = bf16[16,64,4,3,64]{4,3,2,1,0:T(4,128)(2,1)} reshape(bf16[16,64,768]{2,1,0:T(8,128)(2,1)} %convolution_convert_fusion.1) | data formatting | bytes 3145728 | tf_op jit(solution)/shard_map/reshape | solution.py:44
  32.4 1.8 reshape.112
  34.2 3.3 %reshape.114 = bf16[32,64,4,64]{3,2,1,0:T(4,128)(2,1)S(1)} reshape(bf16[32,64,256]{2,1,0:T(8,128)(2,1)} %get-tuple-element.8) | data formatting | bytes 2097152 | tf_op jit(solution)/shard_map/reshape | solution.py:45
  37.5 5.9 %fusion.44 = f32[64,4,16,3,32]{4,2,3,1,0:T(8,128)S(1)} fusion(bf16[16,64,4,3,64]{4,3,2,1,0:T(4,128)(2,1)} %reshape.113, bf16[32,64,4,64,1]{3,2,1,0,4:T(4,128)(2,1)S(1)} %bitcast.75), kind=kOutput, calls=%fused_computation.57 | convolution fusion | flops 50331648 | bytes 4194304 | tf_op jit(solution)/shard_map/tpgrd,spgd->pgtrs/dot_general | solution.py:47
  43.4 4.3 %fusion.101 = (f32[64,4,16,3]{2,3,1,0:T(4,128)S(1)}, f32[64,4,16,3,32]{4,2,3,1,0:T(8,128)S(1)}) fusion(f32[64,4,16,3,32]{4,2,3,1,0:T(8,128)S(1)} %fusion.44, pred[16,32]{1,0:T(8,128)(4,1)S(1)} %fusion.87), kind=kOutput, calls=%fused_computation.105 | output fusion | flops 2359327 | bytes 3195392 | tf_op jit(solution)/shard_map/sub | solution.py:52
  47.7 2.9 %convert_bitcast_fusion = bf16[16,64,4,3,64]{4,0,3,2,1:T(8,128)(2,1)S(1)} fusion(f32[64,4,16,3,32]{4,2,3,1,0:T(8,128)S(1)} %get-tuple-element.12, f32[64,4,16,3]{2,3,1,0:T(4,128)S(1)} %get-tuple-element.11, bf16[32,64,4,64,1]{3,2,1,0,4:T(4,128)(2,1)S(1)} %bitcast.77), kind=kOutput, calls=%fused_computation.59 | convolution fusion | flops 51904512 | bytes 4243456 | tf_op jit(solution)/shard_map/pgtrs,spgd->tpgrd/dot_general | solution.py:54
  50.6 3.8 %copy.23 = bf16[16,64,4,3,64]{4,3,2,1,0:T(4,128)(2,1)} copy(bf16[16,64,4,3,64]{4,0,3,2,1:T(8,128)(2,1)S(1)} %convert_bitcast_fusion) | data formatting | bytes 3145728 | tf_op jit(solution)/shard_map/convert_element_type | solution.py:55
  54.5 8.3 %convert_element_type.80 = bf16[16,64,768]{2,1,0:T(8,128)(2,1)} reshape(bf16[16,64,4,3,64]{4,3,2,1,0:T(4,128)(2,1)} %copy.23) | data formatting | bytes 3145728 | tf_op jit(solution)/shard_map/convert_element_type | solution.py:55
  62.8 2.9 %convert_reduce_fusion.1 = (f32[16,64]{1,0:T(8,128)S(1)}, bf16[16,64,768]{2,1,0:T(8,128)(2,1)S(1)}) fusion(bf16[16,64,768]{2,1,0:T(8,128)(2,1)} %convert_element_type.80, bf16[768,768]{1,0:T(8,128)(2,1)S(1)} %copy-done, bf16[16,64,768]{2,1,0:T(8,128)(2,1)S(1)} %copy-done.3), kind=kOutput, calls=%fused_computation.29 | convolution fusion | flops 1211890688 | bytes 5902336 | tf_op jit(solution)/shard_map/dot_general | solution.py:34
  66.9 2.0 convolution_convert_fusion.2
  69.0 3.3 %convolution_convert_fusion = bf16[16,64,768]{2,1,0:T(8,128)(2,1)S(1)} fusion(bf16[768,768]{1,0:T(8,128)(2,1)} %param.18, bf16[16,64,768]{2,1,0:T(8,128)(2,1)} %copy-done.4, f32[768]{0:T(1024)S(1)} %copy-done.15, f32[16,64]{1,0:T(8,128)S(1)} %add_rsqrt_fusion.1, f32[16,64]{1,0:T(8,128)S(1)} %broadcast_multiply_fusion.1), kind=kOutput, calls=%fused_computation.68 | convolution fusion | flops 1212678144 | bytes 4336640 | tf_op jit(solution)/shard_map/dot_general | solution.py:34
  72.3 5.0 %reshape.117 = bf16[16,64,4,3,64]{4,3,2,1,0:T(4,128)(2,1)} reshape(bf16[16,64,768]{2,1,0:T(8,128)(2,1)S(1)} %convolution_convert_fusion) | data formatting | bytes 3145728 | tf_op jit(solution)/shard_map/vmap()/reshape | solution.py:62
  77.2 76.5 %all-gather.2.cloned.1.call-done = bf16[16,256,512]{2,1,0:T(8,128)(2,1)} async-done(((bf16[16,64,512]{2,1,0:T(8,128)(2,1)}), bf16[16,256,512]{2,1,0:T(8,128)(2,1)}) %all-gather.2.cloned.1.call-update) | async-done | bytes 4194320 | tf_op jit(solution)/shard_map/all_gather | solution.py:106
  153.7 4.6 %fusion.98 = (bf16[16,256,256]{2,1,0:T(8,128)(2,1)}, bf16[16,256,256]{2,1,0:T(8,128)(2,1)}) fusion(bf16[16,256,512]{2,1,0:T(8,128)(2,1)} %all-gather.2.cloned.1.call-done), kind=kLoop, calls=%fused_computation.102 | loop fusion | bytes 8388608 | tf_op jit(solution)/shard_map/vmap()/slice | solution.py:63
  158.4 2.8 %copy.25 = bf16[16,256,256]{1,2,0:T(8,128)(2,1)S(1)} copy(bf16[16,256,256]{2,1,0:T(8,128)(2,1)} %get-tuple-element.5) | data formatting | bytes 4194304 | tf_op jit(solution)/shard_map/vmap()/slice | solution.py:63
  161.2 4.1 %copy.24 = bf16[16,256,256]{1,2,0:T(8,128)(2,1)} copy(bf16[16,256,256]{2,1,0:T(8,128)(2,1)} %get-tuple-element.6) | data formatting | bytes 4194304 | tf_op jit(solution)/shard_map/vmap()/slice | solution.py:64
  165.3 8.5 %fusion.42 = f32[16,4,256,64,3]{2,3,4,1,0:T(8,128)} fusion(bf16[16,256,4,64,1]{1,3,4,2,0:T(8,128)(2,1)S(1)} %bitcast.74, bf16[16,64,4,3,64]{4,3,2,1,0:T(4,128)(2,1)} %reshape.117), kind=kOutput, calls=%fused_computation.55 | convolution fusion | flops 402653184 | bytes 16252928 | tf_op jit(solution)/shard_map/vmap(pgrd,kgd->grpk)/dot_general | solution.py:65
  173.9 12.9 %fusion.102 = f32[16,4,3,64]{3,2,1,0:T(4,128)S(1)} fusion(f32[16,4,256,64,3]{2,3,4,1,0:T(8,128)} %fusion.42), kind=kOutput, calls=%fused_computation.106 | output fusion | flops 12583167 | bytes 12632064 | tf_op jit(solution)/shard_map/vmap()/sub | solution.py:69
  186.8 27.2 %fusion.50 = bf16[16,4,64,3,64]{4,2,3,1,0:T(8,128)(2,1)} fusion(bf16[16,256,4,64,1]{1,3,4,2,0:T(8,128)(2,1)} %bitcast.78, f32[16,4,3,64]{3,2,1,0:T(4,128)S(1)} %fusion.102, f32[16,4,256,64,3]{2,3,4,1,0:T(8,128)} %fusion.42), kind=kOutput, calls=%fused_computation.64 | convolution fusion | flops 419180800 | bytes 16302080 | tf_op jit(solution)/shard_map/vmap(grpk,kgd->pgrd)/dot_general | solution.py:71
  214.0 3.6 %convert_reduce_fusion = (f32[16,64]{1,0:T(8,128)S(1)}, bf16[16,64,768]{2,1,0:T(8,128)(2,1)S(1)}) fusion(bf16[16,64,768]{1,2,0:T(8,128)(2,1)} %bitcast.76, bf16[768,768]{1,0:T(8,128)(2,1)S(1)} %copy-done.10, bf16[16,64,768]{2,1,0:T(8,128)(2,1)S(1)} %copy-done.5), kind=kOutput, calls=%fused_computation.26 | convolution fusion | flops 1211890688 | bytes 5902336 | tf_op jit(solution)/shard_map/dot_general | solution.py:34
  219.3 16.2 %fusion.40 = bf16[16,64,768]{2,1,0:T(8,128)(2,1)} fusion(bf16[16,64,768]{2,1,0:T(8,128)(2,1)} %copy-done.6, bf16[3072,768]{1,0:T(8,128)(2,1)} %param.23, bf16[768,3072]{1,0:T(8,128)(2,1)} %param.22, f32[768]{0:T(1024)S(1)} %copy-done.16, f32[16,64]{1,0:T(8,128)S(1)} %add_rsqrt_fusion, f32[16,64]{1,0:T(8,128)S(1)} %broadcast_multiply_fusion), kind=kOutput, calls=%fused_computation.53 | convolution fusion | flops 9698279424 | bytes 12594176 | tf_op jit(solution)/shard_map/dot_general | solution.py:34
  (55 shorter events, 11.6 us)
Async XLA Ops:
  6.5 56.3 %copy-start = (bf16[768,768]{1,0:T(8,128)(2,1)S(1)}, bf16[768,768]{1,0:T(8,128)(2,1)}, u32[]{:S(2)}) copy-start(bf16[768,768]{1,0:T(8,128)(2,1)} %param.16) | copy-start | bytes 3538948
  6.5 3.9 %copy-start.2 = (bf16[16,64,768]{2,1,0:T(8,128)(2,1)S(1)}, bf16[16,64,768]{2,1,0:T(8,128)(2,1)}, u32[]{:S(2)}) copy-start(bf16[16,64,768]{2,1,0:T(8,128)(2,1)} %param.12) | copy-start | bytes 4718596
  6.5 3.9 %copy-start.14 = (f32[768]{0:T(1024)S(1)}, f32[768]{0:T(1024)}, u32[]{:S(2)}) copy-start(f32[768]{0:T(1024)} %param.13) | copy-start | bytes 9220
  6.5 3.9 %copy-start.12 = (bf16[768,512]{1,0:T(8,128)(2,1)S(1)}, bf16[768,512]{1,0:T(8,128)(2,1)}, u32[]{:S(2)}) copy-start(bf16[768,512]{1,0:T(8,128)(2,1)} %param.15) | copy-start | bytes 2359300
  6.5 147.2 %all-gather.2.cloned.1.call-start = ((), (), s32[]{:S(2)}) async-start(), calls=%async_computation | async-start | bytes 5242880 | tf_op jit(solution)/shard_map/all_gather | solution.py:106
  10.5 7.4 %copy-start.11 = (bf16[768,768]{1,0:T(8,128)(2,1)S(1)}, bf16[768,768]{1,0:T(8,128)(2,1)}, u32[]{:S(2)}) copy-start(bf16[768,768]{1,0:T(8,128)(2,1)} %param.14) | copy-start | bytes 3538948
  11.5 1.0 copy-start.7
  13.4 16.3 %collective-permute-start = (bf16[8,64,512]{2,1,0:T(8,128)(2,1)}, bf16[8,64,512]{2,1,0:T(8,128)(2,1)}, u32[]{:S(2)}, u32[]{:S(2)}) collective-permute-start(bf16[8,64,512]{2,1,0:T(8,128)(2,1)} %get-tuple-element.9), channel_id=1, source_target_pairs={{0,4},{4,8},{8,12},{12,16},{16,20},{20,24},{24,28},{1,5},{5,9},{9,... | collective-permute-start | bytes 1572872 | tf_op jit(solution)/shard_map/ppermute | solution.py:19
  16.5 13.1 %collective-permute-start.1 = (bf16[8,64,512]{2,1,0:T(8,128)(2,1)S(1)}, bf16[8,64,512]{2,1,0:T(8,128)(2,1)}, u32[]{:S(2)}, u32[]{:S(2)}) collective-permute-start(bf16[8,64,512]{2,1,0:T(8,128)(2,1)S(1)} %get-tuple-element.10), channel_id=1, source_target_pairs={{4,0},{8,4},{12,8},{16,12},{20,16},{24,20},{28,24},{5,1},{9,5},{13... | collective-permute-start | bytes 1572872 | tf_op jit(solution)/shard_map/ppermute | solution.py:20
  20.5 9.1 %copy-start.8 = (bf16[16,64,512]{2,1,0:T(8,128)(2,1)S(1)}, bf16[16,64,512]{2,1,0:T(8,128)(2,1)}, u32[]{:S(2)}) copy-start(bf16[16,64,512]{2,1,0:T(8,128)(2,1)} %copy-done.7) | copy-start | bytes 3145732
  43.4 4.3 %copy-start.9 = (bf16[32,64,4,64]{3,2,1,0:T(4,128)(2,1)S(1)}, bf16[32,64,4,64]{3,2,1,0:T(4,128)(2,1)}, u32[]{:S(2)}) copy-start(bf16[32,64,4,64]{3,2,1,0:T(4,128)(2,1)} %reshape.112) | copy-start | bytes 3145732
  54.5 8.4 %copy-start.3 = (bf16[16,64,768]{2,1,0:T(8,128)(2,1)S(1)}, bf16[16,64,768]{2,1,0:T(8,128)(2,1)}, u32[]{:S(2)}) copy-start(bf16[16,64,768]{2,1,0:T(8,128)(2,1)} %param.12) | copy-start | bytes 4718596
  62.8 4.1 %copy-start.13 = (bf16[768,512]{1,0:T(8,128)(2,1)S(1)}, bf16[768,512]{1,0:T(8,128)(2,1)}, u32[]{:S(2)}) copy-start(bf16[768,512]{1,0:T(8,128)(2,1)} %param.19) | copy-start | bytes 2359300
  62.8 4.1 %copy-start.15 = (f32[768]{0:T(1024)S(1)}, f32[768]{0:T(1024)}, u32[]{:S(2)}) copy-start(f32[768]{0:T(1024)} %param.17) | copy-start | bytes 9220
  65.8 1.1 copy-start.4
  186.8 27.2 %copy-start.5 = (bf16[16,64,768]{2,1,0:T(8,128)(2,1)S(1)}, bf16[16,64,768]{2,1,0:T(8,128)(2,1)}, u32[]{:S(2)}) copy-start(bf16[16,64,768]{2,1,0:T(8,128)(2,1)} %copy-done.4) | copy-start | bytes 4718596
  186.8 27.2 %copy-start.10 = (bf16[768,768]{1,0:T(8,128)(2,1)S(1)}, bf16[768,768]{1,0:T(8,128)(2,1)}, u32[]{:S(2)}) copy-start(bf16[768,768]{1,0:T(8,128)(2,1)} %param.20) | copy-start | bytes 3538948
  214.0 5.3 %copy-start.16 = (f32[768]{0:T(1024)S(1)}, f32[768]{0:T(1024)}, u32[]{:S(2)}) copy-start(f32[768]{0:T(1024)} %param.21) | copy-start | bytes 9220
  217.6 1.2 copy-start.6
  219.3 16.2 %copy-start.1 = (bf16[768,768]{1,0:T(8,128)(2,1)S(1)}, bf16[768,768]{1,0:T(8,128)(2,1)}, u32[]{:S(2)}) copy-start(bf16[768,768]{1,0:T(8,128)(2,1)} %param.16) | copy-start | bytes 3538948
Sparse Core Ops, SparseCore 0:
  69.1 84.5 all-gather.1
where the time goes:
time: 247 us; the launch traced here: 243 us
  waiting for transfers between devices  76.5 us (31%)
  matrix products  76.3 us (31%)
  local copies, waits for them, and re-layouts  47.8 us (19%)
  other arithmetic  23.6 us (10%)
  between operations  14 us (6%)
  starting transfers between devices  4.47 us (2%)
    all_gather x1, waiting for transfers between devices, body(): gathered = lax.all_gather(keyvals, 'space', axis=1, tiled=True)  76.5 us
    dot_general x7, matrix products, project(): jnp.dot(flat, w, preferred_element_type=jnp.float32)  31.7 us
    dot_general x1, matrix products, attend_space(): jnp.einsum('grpk,kgd->pgrd', weights, v_heads, preferred_element_type=jnp...  27.2 us
    sub x1, other arithmetic, attend_space(): expo = jnp.exp(scores - top)  12.9 us
    convert_element_type x2, local copies, waits for them, and re-layouts, banded_time(): return out.reshape(count, patches, HEADS * HEAD).astype(jnp.bfloat16)  12.2 us
    reshape x1, local copies, waits for them, and re-layouts, banded_time(): q_heads = queries.reshape(count, patches, KV_HEADS, group, HEAD)  9.09 us
    dot_general x1, matrix products, attend_space(): jnp.einsum('pgrd,kgd->grpk', q_heads, k_heads, preferred_element_type=jnp...  8.54 us
    slice x2, local copies, waits for them, and re-layouts, attend_space(): k_heads = keyvals[:, :KV_HEADS * HEAD].reshape(count, KV_HEADS, HEAD)  7.49 us
  transfers between devices with their start and end apart: 3, of which 1 were waited for; matrix products, arithmetic and copies ran while one was open for 8% of the time, Pallas kernels for 0%

commit v1 on v0

--- a/solution.py
+++ b/solution.py
@@ -7,6 +7,27 @@
 KV_HEADS = 4
 HEAD = 64
 WINDOW = 8
+
+
+def ring_gather(x, axis, dim):
+    size, mine, rows = (lax.axis_size(axis), lax.axis_index(axis), x.shape[dim])
+    forward = [(i, (i + 1) % size) for i in range(size)]
+    left = [(i, (i - 1) % size) for i in range(size)]
+    filled = jnp.zeros((*x.shape[:dim], size * rows, *x.shape[dim + 1 :]), x.dtype)
+    filled = lax.dynamic_update_slice_in_dim(filled, x, mine * rows, axis=dim)
+    from_left = from_right = x
+    half = size // 2
+    for hop in range(1, half + 1):
+        from_left = lax.ppermute(from_left, axis, forward)
+        filled = lax.dynamic_update_slice_in_dim(
+            filled, from_left, (mine - hop) % size * rows, axis=dim
+        )
+        if hop < size - half:
+            from_right = lax.ppermute(from_right, axis, left)
+            filled = lax.dynamic_update_slice_in_dim(
+                filled, from_right, (mine + hop) % size * rows, axis=dim
+            )
+    return filled
 
 
 def extended(x, sides, width):
@@ -103,7 +124,7 @@
     normed = layer_norm(after_time, gain_space)
     queries = project(normed, wq_space).astype(jnp.bfloat16)
     keyvals = project(normed, wkv_space).astype(jnp.bfloat16)
-    gathered = lax.all_gather(keyvals, "space", axis=1, tiled=True)
+    gathered = ring_gather(keyvals, "space", 1)
     attended = jax.vmap(attend_space)(queries, gathered)
     after_space = (after_time.astype(jnp.float32) + project(attended, wo_space)).astype(
         jnp.bfloat16

time: 247 us -> 294 us (1.19)
  the two profiles are of different devices: /device:TPU:0 before, /device:TPU:20 now
where the time goes in v1:
time: 294 us; the launch traced here: 288 us
  local copies, waits for them, and re-layouts  134 us (46%)
  matrix products  74.9 us (25%)
  waiting for transfers between devices  46.3 us (16%)
  other arithmetic  23.6 us (8%)
  starting transfers between devices  8.44 us (3%)
    ppermute x2, waiting for transfers between devices, ring_gather(): from_left = lax.ppermute(from_left, axis, forward)  46.3 us
    dynamic_update_slice x2, local copies, waits for them, and re-layouts, ring_gather(): lax.dynamic_update_slice_in_dim(filled, from_left, (mine - hop) % size *...  41.4 us
    dot_general x7, matrix products, project(): jnp.dot(flat, w, preferred_element_type=jnp.float32)  33 us
    dot_general x1, matrix products, attend_space(): jnp.einsum('grpk,kgd->pgrd', weights, v_heads, preferred_element_type=jnp...  27.1 us
    dynamic_update_slice x1, local copies, waits for them, and re-layouts, ring_gather(): lax.dynamic_update_slice_in_dim(filled, from_right, (mine + hop) % size *...  21 us
    dynamic_update_slice x1, local copies, waits for them, and re-layouts, ring_gather(): filled = lax.dynamic_update_slice_in_dim(filled, x, mine * rows, axis=dim)  17.7 us
    sub x1, other arithmetic, attend_space(): expo = jnp.exp(scores - top)  12.9 us
    convert_element_type x2, local copies, waits for them, and re-layouts, banded_time(): return out.reshape(count, patches, HEADS * HEAD).astype(jnp.bfloat16)  12.2 us
  transfers between devices with their start and end apart: 5, of which 1 were waited for; matrix products, arithmetic and copies ran while one was open for 32% of the time, Pallas kernels for 0%

profile of v1, /device:TPU:20, one launch (start us, length us, event | category | flops | bytes accessed | tf_op | source)
XLA Modules:
  0.0 288.0 jit_solution(17521925085515673007)
XLA Ops:
  5.1 2.8 collective-permute-start.1
  9.8 2.7 convolution_convert_fusion.1
  12.5 8.9 %reshape.113 = bf16[16,64,4,3,64]{4,3,2,1,0:T(4,128)(2,1)} reshape(bf16[16,64,768]{2,1,0:T(8,128)(2,1)} %convolution_convert_fusion.1) | data formatting | bytes 3145728 | tf_op jit(solution)/shard_map/reshape | solution.py:65
  24.5 3.3 %reshape.114 = bf16[32,64,4,64]{3,2,1,0:T(4,128)(2,1)S(1)} reshape(bf16[32,64,256]{2,1,0:T(8,128)(2,1)} %get-tuple-element.8) | data formatting | bytes 2097152 | tf_op jit(solution)/shard_map/reshape | solution.py:66
  27.9 4.4 %reshape.112 = bf16[32,64,4,64]{3,2,1,0:T(4,128)(2,1)} reshape(bf16[32,64,256]{2,1,0:T(8,128)(2,1)} %get-tuple-element.7) | data formatting | bytes 2097152 | tf_op jit(solution)/shard_map/reshape | solution.py:67
  32.3 5.9 %fusion.44 = f32[64,4,16,3,32]{4,2,3,1,0:T(8,128)S(1)} fusion(bf16[16,64,4,3,64]{4,3,2,1,0:T(4,128)(2,1)} %reshape.113, bf16[32,64,4,64,1]{3,2,1,0,4:T(4,128)(2,1)S(1)} %bitcast.75), kind=kOutput, calls=%fused_computation.57 | convolution fusion | flops 50331648 | bytes 4194304 | tf_op jit(solution)/shard_map/tpgrd,spgd->pgtrs/dot_general | solution.py:68
  38.2 4.3 %fusion.101 = (f32[64,4,16,3]{2,3,1,0:T(4,128)S(1)}, f32[64,4,16,3,32]{4,2,3,1,0:T(8,128)S(1)}) fusion(f32[64,4,16,3,32]{4,2,3,1,0:T(8,128)S(1)} %fusion.44, pred[16,32]{1,0:T(8,128)(4,1)S(1)} %fusion.87), kind=kOutput, calls=%fused_computation.105 | output fusion | flops 2359327 | bytes 3195392 | tf_op jit(solution)/shard_map/sub | solution.py:73
  42.5 2.6 convert_bitcast_fusion
  45.1 3.8 %copy.25 = bf16[16,64,4,3,64]{4,3,2,1,0:T(4,128)(2,1)} copy(bf16[16,64,4,3,64]{4,0,3,2,1:T(8,128)(2,1)S(1)} %convert_bitcast_fusion) | data formatting | bytes 3145728 | tf_op jit(solution)/shard_map/convert_element_type | solution.py:76
  48.9 8.3 %convert_element_type.80 = bf16[16,64,768]{2,1,0:T(8,128)(2,1)} reshape(bf16[16,64,4,3,64]{4,3,2,1,0:T(4,128)(2,1)} %copy.25) | data formatting | bytes 3145728 | tf_op jit(solution)/shard_map/convert_element_type | solution.py:76
  57.3 2.9 %convert_reduce_fusion.1 = (f32[16,64]{1,0:T(8,128)S(1)}, bf16[16,64,768]{2,1,0:T(8,128)(2,1)S(1)}) fusion(bf16[16,64,768]{2,1,0:T(8,128)(2,1)} %convert_element_type.80, bf16[768,768]{1,0:T(8,128)(2,1)S(1)} %copy-done, bf16[16,64,768]{2,1,0:T(8,128)(2,1)S(1)} %copy-done.4), kind=kOutput, calls=%fused_computation.29 | convolution fusion | flops 1211890688 | bytes 5902336 | tf_op jit(solution)/shard_map/dot_general | solution.py:55
  64.9 46.3 %collective-permute-done.2 = bf16[16,64,512]{2,1,0:T(8,128)(2,1)S(1)} collective-permute-done((bf16[16,64,512]{2,1,0:T(8,128)(2,1)}, bf16[16,64,512]{2,1,0:T(8,128)(2,1)S(1)}, u32[]{:S(2)}, u32[]{:S(2)}) %collective-permute-start.2) | collective-permute-done | bytes 1048608 | tf_op jit(solution)/shard_map/ppermute | solution.py:21
  114.9 4.4 %convolution_convert_fusion = bf16[16,64,768]{2,1,0:T(8,128)(2,1)} fusion(bf16[768,768]{1,0:T(8,128)(2,1)} %param.18, bf16[16,64,768]{2,1,0:T(8,128)(2,1)} %copy-done.5, f32[768]{0:T(1024)S(1)} %copy-done.14, f32[16,64]{1,0:T(8,128)S(1)} %add_rsqrt_fusion.1, f32[16,64]{1,0:T(8,128)S(1)} %broadcast_multiply_fusion.1), kind=kOutput, calls=%fused_computation.68 | convolution fusion | flops 1212678144 | bytes 4336640 | tf_op jit(solution)/shard_map/dot_general | solution.py:55
  119.4 8.8 %reshape.117 = bf16[16,64,4,3,64]{4,3,2,1,0:T(4,128)(2,1)} reshape(bf16[16,64,768]{2,1,0:T(8,128)(2,1)} %convolution_convert_fusion) | data formatting | bytes 3145728 | tf_op jit(solution)/shard_map/vmap()/reshape | solution.py:83
  130.5 17.7 %dynamic_update_slice.12 = bf16[16,256,512]{1,2,0:T(8,128)(2,1)} dynamic-update-slice(bf16[16,256,512]{1,2,0:T(8,128)(2,1)} %broadcast_in_dim.16, bf16[16,64,512]{1,2,0:T(8,128)(2,1)S(1)} %copy.26, s32[]{:T(128)} %constant.65.clone.1, s32[]{:T(128)S(6)} %select_n.32, s32[]{:T(128)} %constant.65.clone.1) | dynamic-update-slice | bytes 2097156 | tf_op jit(solution)/shard_map/dynamic_update_slice | solution.py:17
  149.3 21.9 %dynamic_update_slice.13 = bf16[16,256,512]{1,2,0:T(8,128)(2,1)} dynamic-update-slice(bf16[16,256,512]{1,2,0:T(8,128)(2,1)} %dynamic_update_slice.12, bf16[16,64,512]{1,2,0:T(8,128)(2,1)S(1)} %copy.27, s32[]{:T(128)} %constant.65.clone.1, s32[]{:T(128)S(6)} %select_n.34, s32[]{:T(128)} %constant.65.clone.1) | dynamic-update-slice | bytes 2097156 | tf_op jit(solution)/shard_map/dynamic_update_slice | solution.py:22
  173.2 21.0 %dynamic_update_slice.14 = bf16[16,256,512]{1,2,0:T(8,128)(2,1)} dynamic-update-slice(bf16[16,256,512]{1,2,0:T(8,128)(2,1)} %dynamic_update_slice.13, bf16[16,64,512]{1,2,0:T(8,128)(2,1)S(1)} %copy.28, s32[]{:T(128)} %constant.65.clone.1, s32[]{:T(128)S(6)} %select_n.36, s32[]{:T(128)} %constant.65.clone.1) | dynamic-update-slice | bytes 2097156 | tf_op jit(solution)/shard_map/dynamic_update_slice | solution.py:27
  196.3 19.4 %dynamic_update_slice.15 = bf16[16,256,512]{1,2,0:T(8,128)(2,1)} dynamic-update-slice(bf16[16,256,512]{1,2,0:T(8,128)(2,1)} %dynamic_update_slice.14, bf16[16,64,512]{1,2,0:T(8,128)(2,1)S(1)} %copy.29, s32[]{:T(128)} %constant.65.clone.1, s32[]{:T(128)S(6)} %select_n.38, s32[]{:T(128)} %constant.65.clone.1) | dynamic-update-slice | bytes 2097156 | tf_op jit(solution)/shard_map/dynamic_update_slice | solution.py:22
  215.8 4.1 %fusion.98 = (bf16[16,256,256]{1,2,0:T(8,128)(2,1)S(1)}, bf16[16,256,256]{1,2,0:T(8,128)(2,1)}) fusion(bf16[16,256,512]{1,2,0:T(8,128)(2,1)} %dynamic_update_slice.15), kind=kLoop, calls=%fused_computation.102 | loop fusion | bytes 8388608 | tf_op jit(solution)/shard_map/vmap()/slice | solution.py:84
  219.8 6.3 %fusion.42 = f32[16,4,256,64,3]{2,3,4,1,0:T(8,128)} fusion(bf16[16,256,4,64,1]{1,3,4,2,0:T(8,128)(2,1)S(1)} %bitcast.74, bf16[16,64,4,3,64]{4,3,2,1,0:T(4,128)(2,1)S(1)} %copy-done.2), kind=kOutput, calls=%fused_computation.55 | convolution fusion | flops 402653184 | bytes 16252928 | tf_op jit(solution)/shard_map/vmap(pgrd,kgd->grpk)/dot_general | solution.py:86
  226.2 12.9 %fusion.102 = f32[16,4,3,64]{3,2,1,0:T(4,128)S(1)} fusion(f32[16,4,256,64,3]{2,3,4,1,0:T(8,128)} %fusion.42), kind=kOutput, calls=%fused_computation.106 | output fusion | flops 12583167 | bytes 12632064 | tf_op jit(solution)/shard_map/vmap()/sub | solution.py:90
  239.1 27.1 %fusion.50 = bf16[16,4,64,3,64]{4,2,3,1,0:T(8,128)(2,1)} fusion(bf16[16,256,4,64,1]{1,3,4,2,0:T(8,128)(2,1)} %bitcast.78, f32[16,4,3,64]{3,2,1,0:T(4,128)S(1)} %fusion.102, f32[16,4,256,64,3]{2,3,4,1,0:T(8,128)} %fusion.42), kind=kOutput, calls=%fused_computation.64 | convolution fusion | flops 419180800 | bytes 16302080 | tf_op jit(solution)/shard_map/vmap(grpk,kgd->pgrd)/dot_general | solution.py:92
  266.2 3.6 %convert_reduce_fusion = (f32[16,64]{1,0:T(8,128)S(1)}, bf16[16,64,768]{2,1,0:T(8,128)(2,1)S(1)}) fusion(bf16[16,64,768]{1,2,0:T(8,128)(2,1)} %bitcast.76, bf16[768,768]{1,0:T(8,128)(2,1)S(1)} %copy-done.9, bf16[16,64,768]{2,1,0:T(8,128)(2,1)S(1)} %copy-done.6), kind=kOutput, calls=%fused_computation.26 | convolution fusion | flops 1211890688 | bytes 5902336 | tf_op jit(solution)/shard_map/dot_general | solution.py:55
  271.6 16.2 %fusion.40 = bf16[16,64,768]{2,1,0:T(8,128)(2,1)} fusion(bf16[16,64,768]{2,1,0:T(8,128)(2,1)} %copy-done.7, bf16[3072,768]{1,0:T(8,128)(2,1)} %param.23, bf16[768,3072]{1,0:T(8,128)(2,1)} %param.22, f32[768]{0:T(1024)S(1)} %copy-done.15, f32[16,64]{1,0:T(8,128)S(1)} %add_rsqrt_fusion, f32[16,64]{1,0:T(8,128)S(1)} %broadcast_multiply_fusion), kind=kOutput, calls=%fused_computation.53 | convolution fusion | flops 9698279424 | bytes 12594176 | tf_op jit(solution)/shard_map/dot_general | solution.py:55
  (63 shorter events, 27.6 us)
Async XLA Ops:
  0.0 57.3 %copy-start = (bf16[768,768]{1,0:T(8,128)(2,1)S(1)}, bf16[768,768]{1,0:T(8,128)(2,1)}, u32[]{:S(2)}) copy-start(bf16[768,768]{1,0:T(8,128)(2,1)} %param.16) | copy-start | bytes 3538948
  0.0 3.9 %copy-start.3 = (bf16[16,64,768]{2,1,0:T(8,128)(2,1)S(1)}, bf16[16,64,768]{2,1,0:T(8,128)(2,1)}, u32[]{:S(2)}) copy-start(bf16[16,64,768]{2,1,0:T(8,128)(2,1)} %param.12) | copy-start | bytes 4718596
  0.0 3.9 %copy-start.13 = (f32[768]{0:T(1024)S(1)}, f32[768]{0:T(1024)}, u32[]{:S(2)}) copy-start(f32[768]{0:T(1024)} %param.13) | copy-start | bytes 9220
  0.0 3.9 %copy-start.11 = (bf16[768,512]{1,0:T(8,128)(2,1)S(1)}, bf16[768,512]{1,0:T(8,128)(2,1)}, u32[]{:S(2)}) copy-start(bf16[768,512]{1,0:T(8,128)(2,1)} %param.15) | copy-start | bytes 2359300
  3.9 5.9 %copy-start.10 = (bf16[768,768]{1,0:T(8,128)(2,1)S(1)}, bf16[768,768]{1,0:T(8,128)(2,1)}, u32[]{:S(2)}) copy-start(bf16[768,768]{1,0:T(8,128)(2,1)} %param.14) | copy-start | bytes 3538948
  5.1 16.4 %collective-permute-start.1 = (bf16[8,64,512]{2,1,0:T(8,128)(2,1)S(1)}, bf16[8,64,512]{2,1,0:T(8,128)(2,1)}, u32[]{:S(2)}, u32[]{:S(2)}) collective-permute-start(bf16[8,64,512]{2,1,0:T(8,128)(2,1)S(1)} %get-tuple-element.10), channel_id=1, source_target_pairs={{4,0},{8,4},{12,8},{16,12},{20,16},{24,20},{28,24},{5,1},{9,5},{13... | collective-permute-start | bytes 1572872 | tf_op jit(solution)/shard_map/ppermute | solution.py:41
  7.8 13.6 %collective-permute-start = (bf16[8,64,512]{2,1,0:T(8,128)(2,1)S(1)}, bf16[8,64,512]{2,1,0:T(8,128)(2,1)}, u32[]{:S(2)}, u32[]{:S(2)}) collective-permute-start(bf16[8,64,512]{2,1,0:T(8,128)(2,1)S(1)} %get-tuple-element.9), channel_id=1, source_target_pairs={{0,4},{4,8},{8,12},{12,16},{16,20},{20,24},{24,28},{1,5},{5,9},{9,... | collective-permute-start | bytes 1572872 | tf_op jit(solution)/shard_map/ppermute | solution.py:40
  38.2 4.3 %copy-start.8 = (bf16[32,64,4,64]{3,2,1,0:T(4,128)(2,1)S(1)}, bf16[32,64,4,64]{3,2,1,0:T(4,128)(2,1)}, u32[]{:S(2)}) copy-start(bf16[32,64,4,64]{3,2,1,0:T(4,128)(2,1)} %reshape.112) | copy-start | bytes 3145732
  48.9 8.4 %copy-start.4 = (bf16[16,64,768]{2,1,0:T(8,128)(2,1)S(1)}, bf16[16,64,768]{2,1,0:T(8,128)(2,1)}, u32[]{:S(2)}) copy-start(bf16[16,64,768]{2,1,0:T(8,128)(2,1)} %param.12) | copy-start | bytes 4718596
  57.3 3.6 %copy-start.12 = (bf16[768,512]{1,0:T(8,128)(2,1)S(1)}, bf16[768,512]{1,0:T(8,128)(2,1)}, u32[]{:S(2)}) copy-start(bf16[768,512]{1,0:T(8,128)(2,1)} %param.19) | copy-start | bytes 2359300
  57.3 3.6 %copy-start.14 = (f32[768]{0:T(1024)S(1)}, f32[768]{0:T(1024)}, u32[]{:S(2)}) copy-start(f32[768]{0:T(1024)} %param.17) | copy-start | bytes 9220
  60.3 2.7 copy-start.5
  62.9 48.3 %collective-permute-start.2 = (bf16[16,64,512]{2,1,0:T(8,128)(2,1)}, bf16[16,64,512]{2,1,0:T(8,128)(2,1)S(1)}, u32[]{:S(2)}, u32[]{:S(2)}) collective-permute-start(bf16[16,64,512]{2,1,0:T(8,128)(2,1)} %convolution_convert_fusion.2), channel_id=1, source_target_pairs={{0,1},{1,2},{2,3},{3,0},{4,5},{5,6},{6,7},{7,4},{8,9},{9,10},{10,1... | collective-permute-start | bytes 3145736 | tf_op jit(solution)/shard_map/ppermute | solution.py:21
  64.5 106.7 %collective-permute-start.3 = (bf16[16,64,512]{2,1,0:T(8,128)(2,1)}, bf16[16,64,512]{2,1,0:T(8,128)(2,1)}, u32[]{:S(2)}, u32[]{:S(2)}) collective-permute-start(bf16[16,64,512]{2,1,0:T(8,128)(2,1)} %convolution_convert_fusion.2), channel_id=1, source_target_pairs={{0,3},{1,0},{2,1},{3,2},{4,7},{5,4},{6,5},{7,6},{8,11},{9,8},{10,9... | collective-permute-start | bytes 3145736 | tf_op jit(solution)/shard_map/ppermute | solution.py:26
  111.2 83.1 %collective-permute-start.4 = (bf16[16,64,512]{2,1,0:T(8,128)(2,1)S(1)}, bf16[16,64,512]{2,1,0:T(8,128)(2,1)}, u32[]{:S(2)}, u32[]{:S(2)}) collective-permute-start(bf16[16,64,512]{2,1,0:T(8,128)(2,1)S(1)} %collective-permute-done.2), channel_id=1, source_target_pairs={{0,1},{1,2},{2,3},{3,0},{4,5},{5,6},{6,7},{7,4},{8,9},{9,10},{10,1... | collective-permute-start | bytes 3145736 | tf_op jit(solution)/shard_map/ppermute | solution.py:21
  215.7 4.1 %copy-start.2 = (bf16[16,64,4,3,64]{4,3,2,1,0:T(4,128)(2,1)S(1)}, bf16[16,64,4,3,64]{4,3,2,1,0:T(4,128)(2,1)}, u32[]{:S(2)}) copy-start(bf16[16,64,4,3,64]{4,3,2,1,0:T(4,128)(2,1)} %reshape.117) | copy-start | bytes 4718596
  239.0 27.2 %copy-start.6 = (bf16[16,64,768]{2,1,0:T(8,128)(2,1)S(1)}, bf16[16,64,768]{2,1,0:T(8,128)(2,1)}, u32[]{:S(2)}) copy-start(bf16[16,64,768]{2,1,0:T(8,128)(2,1)} %copy-done.5) | copy-start | bytes 4718596
  239.0 27.2 %copy-start.9 = (bf16[768,768]{1,0:T(8,128)(2,1)S(1)}, bf16[768,768]{1,0:T(8,128)(2,1)}, u32[]{:S(2)}) copy-start(bf16[768,768]{1,0:T(8,128)(2,1)} %param.20) | copy-start | bytes 3538948
  266.2 5.3 %copy-start.15 = (f32[768]{0:T(1024)S(1)}, f32[768]{0:T(1024)}, u32[]{:S(2)}) copy-start(f32[768]{0:T(1024)} %param.21) | copy-start | bytes 9220
  269.8 1.2 copy-start.7
  271.6 16.2 %copy-start.1 = (bf16[768,768]{1,0:T(8,128)(2,1)S(1)}, bf16[768,768]{1,0:T(8,128)(2,1)}, u32[]{:S(2)}) copy-start(bf16[768,768]{1,0:T(8,128)(2,1)} %param.16) | copy-start | bytes 3538948
